TPU v7x, 256 devices: a whole 4x4x8 slice. The times are simulated.
256 devices in a mesh: kq: 128 (over x, y, z), band: 2 (over core).
Axes of the slice: x: 4, y: 4, z: 8, core: 2. Of those that a mesh axis runs over, the one named last changes fastest.
Arguments:
- orbitals: bfloat16 [128, 16, 4096], P('kq', 'band'), may hold values from -6 to 6
- screening: bfloat16 [256, 1024, 1024], P('kq'), may hold values from -0.1875 to 0.1875
- pair_k: int32 [256, 2], replicated, may hold values from 0 to 127, as said below
- pair_q: int32 [256], P('kq'), may hold values from 0 to 255, as said below
- gmap: int32 [1024], replicated, may hold values from 0 to 4095, as said below
Outputs:
- exch_field: float32 [128, 16, 4096], P('kq', 'band')
Inputs may be any that keep to these rules, and one draw needn't show every extreme that they name: Rows are grouped by owner: rows o * 2 to (o + 1) * 2 - 1 belong to kq index o, and pair_k[o * 2 + i, s] = (pair_k[i, s] + o) mod 128 for every row i of owner 0 and both columns s. The 2 * 2 k-points of one owner are all different, and those of owner 0 include 128 - 1 and 64. `pair_q`: row i names one of the 2 transfers of owner o = i // 2, namely 2 * o to 2 * o + 1, and each of them in 1 of the owner's rows. `gmap`: all entries differ; 0 and 4095 are among them.
All inputs are finite; a program needn't handle non-finite values.
Results may differ from a plain program's by a relative error of at most 0.007.
Values may be sent and summed in bfloat16 or wider, within the bound.
A program may use at most 128 MiB of HBM per device.

v0:
```python
import math
import jax
import jax.numpy as jnp
from jax import lax
from jax.sharding import PartitionSpec as P

GRID = 16


def cas_table(gmap, grid_side):
    cells = grid_side**3
    points = jnp.arange(cells, dtype=jnp.int32)
    coord_x = points // (grid_side * grid_side)
    coord_y = points // grid_side % grid_side
    coord_z = points % grid_side
    freq_x = gmap // (grid_side * grid_side)
    freq_y = gmap // grid_side % grid_side
    freq_z = gmap % grid_side
    phase = (
        freq_x[:, None] * coord_x[None, :]
        + freq_y[:, None] * coord_y[None, :]
        + freq_z[:, None] * coord_z[None, :]
    ) % grid_side
    angle = phase.astype(jnp.float32) * (2.0 * math.pi / grid_side)
    return (jnp.cos(angle) + jnp.sin(angle)).astype(jnp.bfloat16)


def pair_fields(left_block, right_block, screen_mat, table):
    rows_left = left_block.shape[0]
    rows_right = right_block.shape[0]
    cells = table.shape[1]
    factor = 1.0 / math.sqrt(cells)
    density = (
        left_block.astype(jnp.float32)[:, None, :] * right_block.astype(jnp.float32)[None, :, :]
    ).astype(jnp.bfloat16)
    density = density.reshape(rows_left * rows_right, cells)
    spectrum = lax.dot_general(
        density, table, (((1,), (1,)), ((), ())), preferred_element_type=jnp.float32
    )
    spectrum = (spectrum * factor).astype(jnp.bfloat16)
    screened = jnp.dot(spectrum, screen_mat, preferred_element_type=jnp.float32).astype(
        jnp.bfloat16
    )
    potential = (jnp.dot(screened, table, preferred_element_type=jnp.float32) * factor).astype(
        jnp.bfloat16
    )
    potential = potential.reshape(rows_left, rows_right, cells)
    toward_left = jnp.einsum(
        "mnr,nr->mr", potential, right_block, preferred_element_type=jnp.float32
    )
    toward_right = jnp.einsum(
        "mnr,mr->nr", potential, left_block, preferred_element_type=jnp.float32
    )
    return (toward_left, toward_right)


def shards(orbitals, screening, pair_k, pair_q, gmap):
    owner_index = lax.axis_index("kq")
    pair_count = pair_q.shape[0]
    local_pairs = lax.dynamic_slice_in_dim(pair_k, owner_index * pair_count, pair_count, 0)
    first_points = local_pairs[:, 0]
    second_points = local_pairs[:, 1]
    shard_piece = lax.all_gather(orbitals, "kq", axis=0, tiled=True)
    numbers = jnp.arange(shard_piece.shape[0], dtype=jnp.int32)
    pick_first = (first_points[:, None] == numbers[None, :]).astype(jnp.bfloat16)
    pick_second = (second_points[:, None] == numbers[None, :]).astype(jnp.bfloat16)
    first_add = jnp.einsum(
        "pc,cnr->pnr", pick_first, shard_piece, preferred_element_type=jnp.float32
    )
    second_add = jnp.einsum(
        "pc,cnr->pnr", pick_second, shard_piece, preferred_element_type=jnp.float32
    )
    first_half = first_add.astype(jnp.bfloat16)
    second_half = second_add.astype(jnp.bfloat16)
    first_full = lax.all_gather(first_half, "band", axis=1, tiled=True)
    table = cas_table(gmap, GRID)
    screen_slots = pair_q - owner_index * screening.shape[0]

    def one_pair(operands):
        left_block, right_block, screen_slot = operands
        screen_mat = lax.dynamic_index_in_dim(screening, screen_slot, 0, keepdims=False)
        return pair_fields(left_block, right_block, screen_mat, table)

    toward_first, toward_second = lax.map(one_pair, (first_full, second_half, screen_slots))
    first_share = lax.psum_scatter(
        toward_first.astype(jnp.bfloat16), "band", scatter_dimension=1, tiled=True
    ).astype(jnp.float32)
    numbers = jnp.arange(orbitals.shape[0] * lax.axis_size("kq"), dtype=jnp.int32)
    pick_first = (numbers[:, None] == first_points[None, :]).astype(jnp.float32)
    pick_second = (numbers[:, None] == second_points[None, :]).astype(jnp.float32)
    first_term = jnp.einsum("cp,pnr->cnr", pick_first, first_share, precision=lax.Precision.HIGHEST)
    second_term = jnp.einsum(
        "cp,pnr->cnr", pick_second, toward_second, precision=lax.Precision.HIGHEST
    )
    return lax.psum_scatter(first_term + second_term, "kq", scatter_dimension=0, tiled=True)


def solution(mesh):
    in_specs = (P("kq", "band", None), P("kq", None, None), P(), P("kq"), P())
    out_specs = P("kq", "band", None)
    return jax.shard_map(shards, mesh=mesh, in_specs=in_specs, out_specs=out_specs, check_vma=False)
```

profile of v0, /device:TPU:0, one launch (start us, length us, event | category | flops | bytes accessed | tf_op | source)
XLA Modules:
  0.0 1275.1 jit_solution(6615732303375635659)
XLA Ops:
  8.6 1.2 broadcast_subtract_fusion
  10.5 125.8 %all-gather.2.cloned.1.call-done = bf16[128,8,4096]{2,1,0:T(8,128)(2,1)} async-done(((bf16[1,8,4096]{2,1,0:T(8,128)(2,1)}), bf16[128,8,4096]{2,1,0:T(8,128)(2,1)}) %all-gather.2.cloned.1.call-update) | async-done | bytes 8388624 | tf_op jit(solution)/shard_map/all_gather | solution.py:63
  136.4 12.2 fusion.41
  148.7 12.5 fusion.44
  161.1 2.0 all_gather.7
  163.3 322.6 %while.13 = (s32[]{:T(128)}, bf16[2,16,4096]{2,1,0:T(8,128)(2,1)}, f32[2,8,4096]{2,0,1:T(2,128)S(1)}, bf16[2,8,4096]{2,1,0:T(8,128)(2,1)S(1)}, bf16[2,16,4096]{2...) while((s32[]{:T(128)}, bf16[2,16,4096]{2,1,0:T(8,128)(2,1)}, ...), condition=%wide.region_1.2_spmd.clone, body=%wide.region_0.1_spmd.clone.sunk | while | flops 2589425664 | bytes 13951255 | solution.py:84
  177.3 1.3 dynamic_slice.45
  180.5 1.8 fusion.93
  182.3 74.7 %fusion.94 = bf16[128,1024]{1,0:T(8,128)(2,1)} fusion(s32[4096]{0:T(1024)} %get-tuple-element.283, s32[1024]{0:T(1024)S(1)} %get-tuple-element.284, s32[4096]{0:T(1024)} %get-tuple-element.281, s32[1024]{0:T(1024)S(1)} %get-tuple-element.282, s32[4096]{0:T(1024)} %get-tuple-element.279, s32[1024]{0:T(1024)S(1)} %get-tuple-element.280, ...), kind=kOutput, calls=%fused_computation.19.clone.2 | convolution fusion | flops 1427505152 | bytes 2813952 | tf_op jit(solution)/shard_map/while/body/eval_jaxpr/dot_general | solution.py:41
  257.0 72.3 %multiply_reduce_fusion.4 = (bf16[4096,16]{0,1:T(8,128)(2,1)S(1)}, bf16[128,4096]{1,0:T(8,128)(2,1)S(1)}) fusion(f32[4096,8]{0,1:T(8,128)S(1)} %get-tuple-element.234, bf16[128,1024]{1,0:T(8,128)(2,1)} %fusion.94, s32[4096]{0:T(1024)} %get-tuple-element.283, s32[1024]{0:T(1024)S(1)} %get-tuple-element.284, s32[4096]{0:T(1024)} %get-tuple-element.281, ...), kind=kOutput, calls=%fused_computation.15.clone.2 | convolution fusion | flops 1160183808 | bytes 1634304 | tf_op jit(solution)/shard_map/while/body/eval_jaxpr/dot_general | solution.py:44
  329.7 1.1 dynamic_update_slice.14
  331.5 1.3 dynamic_slice.45
  334.7 1.8 fusion.93
  336.5 74.7 %fusion.94 = bf16[128,1024]{1,0:T(8,128)(2,1)} fusion(s32[4096]{0:T(1024)} %get-tuple-element.283, s32[1024]{0:T(1024)S(1)} %get-tuple-element.284, s32[4096]{0:T(1024)} %get-tuple-element.281, s32[1024]{0:T(1024)S(1)} %get-tuple-element.282, s32[4096]{0:T(1024)} %get-tuple-element.279, s32[1024]{0:T(1024)S(1)} %get-tuple-element.280, ...), kind=kOutput, calls=%fused_computation.19.clone.2 | convolution fusion | flops 1427505152 | bytes 2813952 | tf_op jit(solution)/shard_map/while/body/eval_jaxpr/dot_general | solution.py:41
  411.2 72.3 %multiply_reduce_fusion.4 = (bf16[4096,16]{0,1:T(8,128)(2,1)S(1)}, bf16[128,4096]{1,0:T(8,128)(2,1)S(1)}) fusion(f32[4096,8]{0,1:T(8,128)S(1)} %get-tuple-element.234, bf16[128,1024]{1,0:T(8,128)(2,1)} %fusion.94, s32[4096]{0:T(1024)} %get-tuple-element.283, s32[1024]{0:T(1024)S(1)} %get-tuple-element.284, s32[4096]{0:T(1024)} %get-tuple-element.281, ...), kind=kOutput, calls=%fused_computation.15.clone.2 | convolution fusion | flops 1160183808 | bytes 1634304 | tf_op jit(solution)/shard_map/while/body/eval_jaxpr/dot_general | solution.py:44
  483.8 1.1 dynamic_update_slice.14
  485.9 1.2 copy.31
  487.1 0.9 copy.39
  488.0 10.0 reduce-scatter.7.cloned.1.call-done
  498.0 1.0 reshape.72
  499.0 3.0 fusion.47
  502.0 10.5 convolution_add_fusion
  512.6 17.7 %copy.18 = f32[128,8,4096]{2,1,0:T(8,128)} copy(f32[128,8,4096]{2,0,1:T(8,128)} %convolution_add_fusion) | data formatting | bytes 33554432 | tf_op jit(solution)/shard_map/add | solution.py:95
  530.3 737.9 %reduce-scatter.5.cloned.1.call-done = f32[1,8,4096]{2,1,0:T(8,128)} async-done(((f32[128,8,4096]{2,1,0:T(8,128)}), f32[1,8,4096]{2,1,0:T(8,128)}) %reduce-scatter.5.cloned.1.call-update) | async-done | bytes 131088 | tf_op jit(solution)/shard_map/reduce_scatter | solution.py:95
  (43 shorter events, 5.4 us)
Async XLA Ops:
  6.5 0.8 copy-start
  6.5 129.8 %all-gather.2.cloned.1.call-start = ((), (), s32[]{:S(2)}) async-start(), calls=%async_computation.2 | async-start | bytes 8454144 | tf_op jit(solution)/shard_map/all_gather | solution.py:63
  7.3 490.8 %reduce-scatter.7.cloned.1.call-start = ((), (), s32[]{:S(2)}) async-start(), calls=%async_computation.4 | async-start | bytes 393216
  9.8 126.5 %copy-start.5 = (s32[2]{0:T(128)}, s32[2]{0:T(128)S(1)}, u32[]{:S(2)}) copy-start(s32[2]{0:T(128)S(1)} %get-tuple-element.146) | copy-start | bytes 28
  9.8 153.4 %copy-start.4 = (s32[2]{0:T(128)}, s32[2]{0:T(128)S(1)}, u32[]{:S(2)}) copy-start(s32[2]{0:T(128)S(1)} %get-tuple-element.145) | copy-start | bytes 28
  257.0 73.7 %copy-start.2 = (bf16[2,16,4096]{2,1,0:T(8,128)(2,1)S(1)}, bf16[2,16,4096]{2,1,0:T(8,128)(2,1)}, u32[]{:S(2)}) copy-start(bf16[2,16,4096]{2,1,0:T(8,128)(2,1)} %get-tuple-element.257) | copy-start | bytes 786436 | tf_op jit(solution)/shard_map/while
  330.8 0.7 copy-start.3
  411.2 73.7 %copy-start.2 = (bf16[2,16,4096]{2,1,0:T(8,128)(2,1)S(1)}, bf16[2,16,4096]{2,1,0:T(8,128)(2,1)}, u32[]{:S(2)}) copy-start(bf16[2,16,4096]{2,1,0:T(8,128)(2,1)} %get-tuple-element.257) | copy-start | bytes 786436 | tf_op jit(solution)/shard_map/while
  485.0 0.7 copy-start.3
  485.9 16.2 %copy-start.6 = (s32[2]{0:T(128)S(1)}, s32[2]{0:T(128)}, u32[]{:S(2)}) copy-start(s32[2]{0:T(128)} %copy-done.5) | copy-start | bytes 28
  488.0 780.2 %reduce-scatter.5.cloned.1.call-start = ((), (), s32[]{:S(2)}) async-start(), calls=%async_computation.3 | async-start | bytes 16908288 | tf_op jit(solution)/shard_map/reduce_scatter | solution.py:95
  512.5 755.7 %copy-start.1 = (s32[256,2]{0,1:T(2,128)S(1)}, s32[256,2]{0,1:T(2,128)}, u32[]{:S(2)}) copy-start(s32[256,2]{0,1:T(2,128)} %param.9) | copy-start | bytes 6148
Sparse Core Ops, SparseCore 0:
  11.0 125.3 all-gather.1
  488.1 9.8 reduce-scatter.6
  530.4 737.7 reduce-scatter.4
where the time goes:
time: 1280 us
  waiting for transfers between devices  874 us (68%)
  matrix products  332 us (26%)
  local copies, waits for them, and re-layouts  31 us (2%)
  loops' own time  18.1 us (1%)
  between operations  13.6 us (1%)
    reduce_scatter x1, waiting for transfers between devices, shards(): lax.psum_scatter(first_term + second_term, 'kq', scatter_dimension=0, til...  738 us
    dot_general x2, matrix products, pair_fields(): jnp.dot(spectrum, screen_mat, preferred_element_type=jnp.float32)  149 us
    dot_general x2, matrix products, pair_fields(): jnp.dot(screened, table, preferred_element_type=jnp.float32) * factor  145 us
    all_gather x1, waiting for transfers between devices, shards(): shard_piece = lax.all_gather(orbitals, 'kq', axis=0, tiled=True)  126 us
  transfers between devices with their start and end apart: 3, of which 3 were waited for; matrix products, arithmetic and copies ran while one was open for 0% of the time, Pallas kernels for 0%

commit v1 on v0

--- a/solution.py
+++ b/solution.py
@@ -60,7 +60,9 @@
     local_pairs = lax.dynamic_slice_in_dim(pair_k, owner_index * pair_count, pair_count, 0)
     first_points = local_pairs[:, 0]
     second_points = local_pairs[:, 1]
-    shard_piece = lax.all_gather(orbitals, "kq", axis=0, tiled=True)
+    shard_piece = jnp.concatenate(
+        lax.all_to_all(jnp.stack([orbitals] * lax.axis_size("kq")), "kq", 0, 0), axis=0
+    )
     numbers = jnp.arange(shard_piece.shape[0], dtype=jnp.int32)
     pick_first = (first_points[:, None] == numbers[None, :]).astype(jnp.bfloat16)
     pick_second = (second_points[:, None] == numbers[None, :]).astype(jnp.bfloat16)

time: 1280 us -> 1340 us (1.047)
  waiting for transfers between devices: 874 us -> 928 us
  starting transfers between devices: 0.08 us -> 14.9 us
    all_to_all x0 -> x1, waiting for transfers between devices: none -> 187 us  [shards(): lax.all_to_all(jnp.stack([orbitals] * lax.axis_size('kq')), 'kq', 0, 0)]
    all_gather x1 -> x0, waiting for transfers between devices: 126 us -> none  [shards(): shard_piece = lax.all_gather(orbitals, 'kq', axis=0, tiled=True)]
    all_to_all x0 -> x1, starting transfers between devices: none -> 14.6 us  [shards(): lax.all_to_all(jnp.stack([orbitals] * lax.axis_size('kq')), 'kq', 0, 0)]
where the time goes in v1:
time: 1340 us
  waiting for transfers between devices  928 us (69%)
  matrix products  332 us (25%)
  local copies, waits for them, and re-layouts  36.2 us (3%)
  starting transfers between devices  14.9 us (1%)
  between operations  13.7 us (1%)
    reduce_scatter x1, waiting for transfers between devices, shards(): lax.psum_scatter(first_term + second_term, 'kq', scatter_dimension=0, til...  737 us
    all_to_all x1, waiting for transfers between devices, shards(): lax.all_to_all(jnp.stack([orbitals] * lax.axis_size('kq')), 'kq', 0, 0)  187 us
    dot_general x2, matrix products, pair_fields(): jnp.dot(spectrum, screen_mat, preferred_element_type=jnp.float32)  149 us
    dot_general x2, matrix products, pair_fields(): jnp.dot(screened, table, preferred_element_type=jnp.float32) * factor  145 us
  transfers between devices with their start and end apart: 3, of which 3 were waited for; matrix products, arithmetic and copies ran while one was open for 0% of the time, Pallas kernels for 0%

profile of v1, /device:TPU:0, one launch (start us, length us, event | category | flops | bytes accessed | tf_op | source)
XLA Modules:
  0.0 1339.5 jit_solution(13338060155266919179)
XLA Ops:
  6.5 5.2 stack.2
  11.7 14.6 %all-to-all-start = ((bf16[128,1,8,4096]{3,2,1,0:T(8,128)(2,1)}), bf16[128,1,8,4096]{3,2,1,0:T(8,128)(2,1)}, u32[]{:S(2)}, u32[]{:S(2)}) async-start(bf16[128,1,8,4096]{3,2,1,0:T(8,128)(2,1)} %stack.2), calls=%async_computation | async-start | bytes 16777216 | tf_op jit(solution)/shard_map/all_to_all | solution.py:64
  28.5 186.6 %all-to-all-done = bf16[128,1,8,4096]{3,2,1,0:T(8,128)(2,1)} async-done(((bf16[128,1,8,4096]{3,2,1,0:T(8,128)(2,1)}), bf16[128,1,8,4096]{3,2,1,0:T(8,128)(2,1)}, u32[]{:S(2)}, u32[]{:S(2)}) %all-to-all-start) | async-done | bytes 8388640 | tf_op jit(solution)/shard_map/all_to_all | solution.py:64
  215.1 12.2 fusion.43
  227.4 12.6 fusion.46
  240.0 2.0 all_gather.3
  242.2 313.9 %while.13 = (s32[]{:T(128)}, bf16[2,16,4096]{2,1,0:T(8,128)(2,1)}, f32[2,8,4096]{2,0,1:T(2,128)S(1)}, bf16[2,8,4096]{2,1,0:T(8,128)(2,1)S(1)}, bf16[2,16,4096]{2...) while((s32[]{:T(128)}, bf16[2,16,4096]{2,1,0:T(8,128)(2,1)}, ...), condition=%wide.region_1.2_spmd.clone, body=%wide.region_0.1_spmd.clone.sunk | while | flops 2589425664 | bytes 13951255 | solution.py:86
  247.4 1.3 dynamic_slice.45
  250.7 1.8 fusion.95
  252.5 74.7 %fusion.96 = bf16[128,1024]{1,0:T(8,128)(2,1)} fusion(s32[4096]{0:T(1024)} %get-tuple-element.283, s32[1024]{0:T(1024)S(1)} %get-tuple-element.284, s32[4096]{0:T(1024)} %get-tuple-element.281, s32[1024]{0:T(1024)S(1)} %get-tuple-element.282, s32[4096]{0:T(1024)} %get-tuple-element.279, s32[1024]{0:T(1024)S(1)} %get-tuple-element.280, ...), kind=kOutput, calls=%fused_computation.19.clone.2 | convolution fusion | flops 1427505152 | bytes 2813952 | tf_op jit(solution)/shard_map/while/body/eval_jaxpr/dot_general | solution.py:41
  327.2 72.3 %multiply_reduce_fusion.4 = (bf16[4096,16]{0,1:T(8,128)(2,1)S(1)}, bf16[128,4096]{1,0:T(8,128)(2,1)S(1)}) fusion(f32[4096,8]{0,1:T(8,128)S(1)} %get-tuple-element.234, bf16[128,1024]{1,0:T(8,128)(2,1)} %fusion.96, s32[4096]{0:T(1024)} %get-tuple-element.283, s32[1024]{0:T(1024)S(1)} %get-tuple-element.284, s32[4096]{0:T(1024)} %get-tuple-element.281, ...), kind=kOutput, calls=%fused_computation.15.clone.2 | convolution fusion | flops 1160183808 | bytes 1634304 | tf_op jit(solution)/shard_map/while/body/eval_jaxpr/dot_general | solution.py:44
  399.8 1.1 dynamic_update_slice.14
  401.7 1.3 dynamic_slice.45
  405.0 1.8 fusion.95
  406.7 74.7 %fusion.96 = bf16[128,1024]{1,0:T(8,128)(2,1)} fusion(s32[4096]{0:T(1024)} %get-tuple-element.283, s32[1024]{0:T(1024)S(1)} %get-tuple-element.284, s32[4096]{0:T(1024)} %get-tuple-element.281, s32[1024]{0:T(1024)S(1)} %get-tuple-element.282, s32[4096]{0:T(1024)} %get-tuple-element.279, s32[1024]{0:T(1024)S(1)} %get-tuple-element.280, ...), kind=kOutput, calls=%fused_computation.19.clone.2 | convolution fusion | flops 1427505152 | bytes 2813952 | tf_op jit(solution)/shard_map/while/body/eval_jaxpr/dot_general | solution.py:41
  481.4 72.3 %multiply_reduce_fusion.4 = (bf16[4096,16]{0,1:T(8,128)(2,1)S(1)}, bf16[128,4096]{1,0:T(8,128)(2,1)S(1)}) fusion(f32[4096,8]{0,1:T(8,128)S(1)} %get-tuple-element.234, bf16[128,1024]{1,0:T(8,128)(2,1)} %fusion.96, s32[4096]{0:T(1024)} %get-tuple-element.283, s32[1024]{0:T(1024)S(1)} %get-tuple-element.284, s32[4096]{0:T(1024)} %get-tuple-element.281, ...), kind=kOutput, calls=%fused_computation.15.clone.2 | convolution fusion | flops 1160183808 | bytes 1634304 | tf_op jit(solution)/shard_map/while/body/eval_jaxpr/dot_general | solution.py:44
  554.1 1.1 dynamic_update_slice.14
  556.1 1.2 copy.29
  558.3 4.8 reduce-scatter.7.cloned.1.call-done
  563.1 1.0 reshape.79
  564.1 3.0 fusion.49
  567.2 10.5 convolution_add_fusion
  577.7 17.7 %copy.16 = f32[128,8,4096]{2,1,0:T(8,128)} copy(f32[128,8,4096]{2,0,1:T(8,128)} %convolution_add_fusion) | data formatting | bytes 33554432 | tf_op jit(solution)/shard_map/add | solution.py:97
  595.4 737.0 %reduce-scatter.5.cloned.1.call-done = f32[1,8,4096]{2,1,0:T(8,128)} async-done(((f32[128,8,4096]{2,1,0:T(8,128)}), f32[1,8,4096]{2,1,0:T(8,128)}) %reduce-scatter.5.cloned.1.call-update) | async-done | bytes 131088 | tf_op jit(solution)/shard_map/reduce_scatter | solution.py:97
  (47 shorter events, 5.6 us)
Async XLA Ops:
  6.5 20.0 %copy-start = (s32[256,2]{0,1:T(2,128)S(1)}, s32[256,2]{0,1:T(2,128)}, u32[]{:S(2)}) copy-start(s32[256,2]{0,1:T(2,128)} %param.9) | copy-start | bytes 6148
  6.5 21.3 %copy-start.8 = (s32[2]{0:T(128)S(1)}, s32[2]{0:T(128)}, u32[]{:S(2)}) copy-start(s32[2]{0:T(128)} %param.10) | copy-start | bytes 28
  6.5 21.9 %copy-start.7 = (s32[1024]{0:T(1024)S(1)}, s32[1024]{0:T(1024)}, u32[]{:S(2)}) copy-start(s32[1024]{0:T(1024)} %param.11) | copy-start | bytes 12292
  11.7 203.4 %all-to-all-start = ((bf16[128,1,8,4096]{3,2,1,0:T(8,128)(2,1)}), bf16[128,1,8,4096]{3,2,1,0:T(8,128)(2,1)}, u32[]{:S(2)}, u32[]{:S(2)}) async-start(bf16[128,1,8,4096]{3,2,1,0:T(8,128)(2,1)} %stack.2), calls=%async_computation | async-start | bytes 16777216 | tf_op jit(solution)/shard_map/all_to_all | solution.py:64
  26.3 536.8 %reduce-scatter.7.cloned.1.call-start = ((), (), s32[]{:S(2)}) async-start(), calls=%async_computation.4 | async-start | bytes 393216
  28.5 186.6 %copy-start.5 = (s32[2]{0:T(128)}, s32[2]{0:T(128)S(1)}, u32[]{:S(2)}) copy-start(s32[2]{0:T(128)S(1)} %get-tuple-element.146) | copy-start | bytes 28
  28.5 213.7 %copy-start.4 = (s32[2]{0:T(128)}, s32[2]{0:T(128)S(1)}, u32[]{:S(2)}) copy-start(s32[2]{0:T(128)S(1)} %get-tuple-element.145) | copy-start | bytes 28
  327.2 73.7 %copy-start.2 = (bf16[2,16,4096]{2,1,0:T(8,128)(2,1)S(1)}, bf16[2,16,4096]{2,1,0:T(8,128)(2,1)}, u32[]{:S(2)}) copy-start(bf16[2,16,4096]{2,1,0:T(8,128)(2,1)} %get-tuple-element.257) | copy-start | bytes 786436 | tf_op jit(solution)/shard_map/while
  401.0 0.7 copy-start.3
  481.4 73.7 %copy-start.2 = (bf16[2,16,4096]{2,1,0:T(8,128)(2,1)S(1)}, bf16[2,16,4096]{2,1,0:T(8,128)(2,1)}, u32[]{:S(2)}) copy-start(bf16[2,16,4096]{2,1,0:T(8,128)(2,1)} %get-tuple-element.257) | copy-start | bytes 786436 | tf_op jit(solution)/shard_map/while
  555.2 0.7 copy-start.3
  556.1 11.0 copy-start.6
  558.2 774.2 %reduce-scatter.5.cloned.1.call-start = ((), (), s32[]{:S(2)}) async-start(), calls=%async_computation.3 | async-start | bytes 16908288 | tf_op jit(solution)/shard_map/reduce_scatter | solution.py:97
  577.7 754.7 %copy-start.1 = (s32[256,2]{0,1:T(2,128)S(1)}, s32[256,2]{0,1:T(2,128)}, u32[]{:S(2)}) copy-start(s32[256,2]{0,1:T(2,128)} %param.9) | copy-start | bytes 6148
Sparse Core Ops, SparseCore 0:
  558.3 4.7 reduce-scatter.6
  595.5 736.8 reduce-scatter.4
